TPU v7x, 32 devices: a whole 2x2x4 slice. The times are simulated.
32 devices in a mesh: dp: 4 (over z), section: 2 (over x), mp: 4 (over y, core).
Axes of the slice: x: 2, y: 2, z: 4, core: 2. Of those that a mesh axis runs over, the one named last changes fastest.
Arguments:
- source_rows: bfloat16 [1024, 1024], P('dp', 'mp'), may hold values from -6 to 6
- value_weight: bfloat16 [2, 1024, 1024], P('section', None, 'mp'), may hold values from -0.1875 to 0.1875
- gate_weight: bfloat16 [2, 1024, 1024], P('section', None, 'mp'), may hold values from -0.1875 to 0.1875
- kernel_weight: bfloat16 [2, 1024, 496], P('section', None, 'mp'), may hold values from -0.1875 to 0.1875
- segment_ids: int32 [8, 128], P('dp'), may hold values from 0 to 3, never falling along the last dimension, each value on 1 to 64 neighbouring positions
- out_grad: bfloat16 [1024, 1024], P('dp', 'mp'), may hold values from -6 to 6
Outputs:
- value_grad: float32 [2, 1024, 1024], P('section', 'dp', 'mp')
- gate_grad: float32 [2, 1024, 1024], P('section', 'dp', 'mp')
- kernel_grad: float32 [2, 1024, 496], P('section', 'dp', 'mp')
Inputs may be any that keep to these rules, and one draw needn't show every extreme that they name: `segment_ids`: in each microbatch row of 128 positions the sentence numbers never fall and every number from 0 up to the largest appears; a sentence covers 1 to 64 positions, and in every microbatch exactly one sentence covers 64 positions.
All inputs are finite; a program needn't handle non-finite values.
Results may differ from a plain program's by a relative error of at most 0.015.
Values may be sent and summed in bfloat16 or wider, within the bound.
A program may use at most 64 MiB of HBM per device.

v0:
```python
import jax
import jax.numpy as jnp
from jax import lax
from jax.sharding import PartitionSpec as P

KERNEL = 31


def from_behind(value, axis, steps):
    count = lax.axis_size(axis)
    initial, last = (max(0, -steps), min(count, count - steps))
    return lax.ppermute(value, axis, [(source, source + steps) for source in range(initial, last)])


def make_table(segments):
    row_count = segments.shape[0]
    positions = jnp.arange(row_count, dtype=jnp.int32)
    offsets = positions[None, :] - positions[:, None] + KERNEL // 2
    same_doc = segments[:, None] == segments[None, :]
    tap_index = jnp.arange(KERNEL, dtype=jnp.int32)[:, None, None]
    return ((offsets[None] == tap_index) & same_doc[None]).astype(jnp.float32)


def normalize(rows_in):
    widened = rows_in.astype(jnp.float32)
    row_mean = jnp.mean(widened, axis=-1, keepdims=True)
    centred = widened - row_mean
    inv_std = lax.rsqrt(jnp.mean(centred * centred, axis=-1, keepdims=True) + 1e-05)
    normed = centred * inv_std
    return (normed, inv_std, normed.astype(jnp.bfloat16))


def forward_pieces(normed_b, band_table, weights):
    w_value, w_gate, w_kernel = weights
    row_count = normed_b.shape[0]
    value_proj = jnp.dot(normed_b, w_value, preferred_element_type=jnp.float32)
    gate_proj = jnp.dot(normed_b, w_gate, preferred_element_type=jnp.float32)
    gate_sig = jax.nn.sigmoid(gate_proj)
    gated = (value_proj * gate_sig).astype(jnp.bfloat16)
    head_count = w_kernel.shape[1] // KERNEL
    head_size = w_value.shape[1] // head_count
    logits = jnp.dot(normed_b, w_kernel, preferred_element_type=jnp.float32).reshape(
        row_count, head_count, KERNEL
    )
    exp_logits = jnp.exp(logits)
    taps = exp_logits / jnp.sum(exp_logits, axis=-1, keepdims=True)
    band_mat = jnp.einsum(
        "thj,jts->hts",
        taps.astype(jnp.bfloat16),
        band_table.astype(jnp.bfloat16),
        preferred_element_type=jnp.float32,
    ).astype(jnp.bfloat16)
    gated3 = gated.reshape(row_count, head_count, head_size)
    mixed = jnp.einsum(
        "hts,shd->thd", band_mat, gated3, preferred_element_type=jnp.float32
    ).reshape(row_count, -1)
    return (value_proj, gate_sig, gated3, taps, band_mat, mixed)


def layer_forward(full_rows, segments, weights, mp_index):
    normed, inv_std, normed_b = normalize(full_rows)
    pieces = forward_pieces(normed_b, make_table(segments), weights)
    half_width = weights[0].shape[1]
    own_part = lax.dynamic_slice_in_dim(
        full_rows.astype(jnp.float32), mp_index * half_width, half_width, 1
    )
    return (own_part + pieces[5]).astype(jnp.bfloat16)


def layer_backward(normed_b, segments, grad_out, weights):
    w_value, w_gate, w_kernel = weights
    band_table = make_table(segments)
    value_proj, gate_sig, gated3, taps, band_mat, mixed = forward_pieces(
        normed_b, band_table, weights
    )
    row_count, head_count, head_size = gated3.shape
    grad_mixed = grad_out.astype(jnp.bfloat16).reshape(row_count, head_count, head_size)
    grad_gated = jnp.einsum(
        "hts,thd->shd", band_mat, grad_mixed, preferred_element_type=jnp.float32
    ).reshape(row_count, -1)
    tap_outer = jnp.einsum("thd,shd->hts", grad_mixed, gated3, preferred_element_type=jnp.float32)
    grad_taps = jnp.einsum("hts,jts->thj", tap_outer, band_table)
    grad_logits = (
        (taps * (grad_taps - jnp.sum(taps * grad_taps, axis=-1, keepdims=True)))
        .astype(jnp.bfloat16)
        .reshape(row_count, -1)
    )
    grad_value = (grad_gated * gate_sig).astype(jnp.bfloat16)
    grad_gate = (grad_gated * value_proj * gate_sig * (1.0 - gate_sig)).astype(jnp.bfloat16)
    dims = (((1,), (1,)), ((), ()))
    grad_part = lax.dot_general(grad_value, w_value, dims, preferred_element_type=jnp.float32)
    grad_part = grad_part + lax.dot_general(
        grad_gate, w_gate, dims, preferred_element_type=jnp.float32
    )
    grad_part = grad_part + lax.dot_general(
        grad_logits, w_kernel, dims, preferred_element_type=jnp.float32
    )
    return (grad_part, jnp.concatenate([grad_value, grad_gate, grad_logits], axis=1))


def shards(source_rows, value_weight, gate_weight, kernel_weight, segment_ids, out_grad):
    section_count = lax.axis_size("section")
    section_index = lax.axis_index("section")
    mp_index = lax.axis_index("mp")
    micro_count, row_count = segment_ids.shape
    full_width = value_weight.shape[1]
    half_width = value_weight.shape[2]
    weights = (value_weight[0], gate_weight[0], kernel_weight[0])
    term_width = 2 * half_width + kernel_weight.shape[2]
    inputs = source_rows.reshape(micro_count, row_count, half_width)
    top_grads = out_grad.reshape(micro_count, row_count, half_width)
    tick_count = micro_count + section_count - 1

    def forward_tick(tick, carry):
        received, stored = carry
        micro_index = tick - section_index
        active = (micro_index >= 0) & (micro_index < micro_count)
        slot_index = jnp.clip(micro_index, 0, micro_count - 1)
        own_rows = jnp.where(section_index == 0, inputs[slot_index], received)
        full_rows = lax.all_gather(own_rows, "mp", axis=1, tiled=True)
        segments = segment_ids[slot_index]
        result = lax.cond(
            active,
            lambda: layer_forward(full_rows, segments, weights, mp_index),
            lambda: jnp.zeros_like(own_rows),
        )
        stored = stored.at[slot_index].set(jnp.where(active, full_rows, stored[slot_index]))
        passed = from_behind(result, "section", 1)
        return (passed, stored)

    start_rows = jnp.zeros((row_count, half_width), jnp.bfloat16)
    start_store = jnp.zeros((micro_count, row_count, full_width), jnp.bfloat16)
    unused, stored = lax.fori_loop(0, tick_count, forward_tick, (start_rows, start_store))

    def backward_tick(tick, carry):
        received, grads, terms_store = carry
        micro_index = tick - (section_count - 1 - section_index)
        active = (micro_index >= 0) & (micro_index < micro_count)
        slot_index = jnp.clip(micro_index, 0, micro_count - 1)
        top_grad = top_grads[slot_index].astype(jnp.float32)
        grad_out = jnp.where(section_index == section_count - 1, top_grad, received)
        segments = segment_ids[slot_index]
        normed, inv_std, normed_b = normalize(stored[slot_index])
        grad_part, grad_terms = lax.cond(
            active,
            lambda: layer_backward(normed_b, segments, grad_out, weights),
            lambda: (
                jnp.zeros((row_count, full_width), jnp.float32),
                jnp.zeros((row_count, term_width), jnp.bfloat16),
            ),
        )
        grad_normed = lax.psum(grad_part.astype(jnp.bfloat16), "mp").astype(jnp.float32)
        norm_back = inv_std * (
            grad_normed
            - jnp.mean(grad_normed, axis=-1, keepdims=True)
            - normed * jnp.mean(grad_normed * normed, axis=-1, keepdims=True)
        )
        own_back = lax.dynamic_slice_in_dim(norm_back, mp_index * half_width, half_width, 1)
        grad_in = grad_out + own_back
        grad_in = jnp.where(active, grad_in, 0.0)
        grads = lax.cond(
            active,
            lambda: grads
            + lax.dot_general(
                normed_b, grad_terms, (((0,), (0,)), ((), ())), preferred_element_type=jnp.float32
            ),
            lambda: grads,
        )
        passed = from_behind(grad_in.astype(jnp.bfloat16), "section", -1).astype(grad_in.dtype)
        return (passed, grads, terms_store)

    start_grads = jnp.zeros((full_width, term_width), jnp.float32)
    start_terms = jnp.zeros((1,), jnp.bfloat16)
    start_back = jnp.zeros((row_count, half_width), jnp.float32)
    unused, grads, terms_store = lax.fori_loop(
        0, tick_count, backward_tick, (start_back, start_grads, start_terms)
    )
    shares = lax.psum_scatter(
        grads.astype(jnp.bfloat16), "dp", scatter_dimension=0, tiled=True
    ).astype(jnp.float32)
    value_share = shares[:, :half_width][None]
    gate_share = shares[:, half_width : 2 * half_width][None]
    kernel_share = shares[:, 2 * half_width :][None]
    return (value_share, gate_share, kernel_share)


def solution(mesh):
    in_specs = (
        P("dp", "mp"),
        P("section", None, "mp"),
        P("section", None, "mp"),
        P("section", None, "mp"),
        P("dp", None),
        P("dp", "mp"),
    )
    out_specs = (P("section", "dp", "mp"), P("section", "dp", "mp"), P("section", "dp", "mp"))
    return jax.shard_map(shards, mesh=mesh, in_specs=in_specs, out_specs=out_specs, check_vma=False)
```

profile of v0, /device:TPU:0, one launch (start us, length us, event | category | flops | bytes accessed | tf_op | source)
XLA Modules:
  0.0 359.8 jit_solution(7524102810339772016)
XLA Ops:
  8.1 50.1 %while.38 = (s32[]{:T(128)}, bf16[128,256]{0,1:T(8,128)(2,1)S(1)}, bf16[2,128,1024]{1,2,0:T(8,128)(2,1)S(1)}, s32[]{:T(128)}, pred[]{:T(512)}, /*index=5*/bf16[2...) while((s32[]{:T(128)}, bf16[128,256]{0,1:T(8,128)(2,1)S(1)}, ...), condition=%wide.region_7.8_spmd, body=%wide.region_0.7_spmd.sunk | while | flops 184383632 | bytes 11819549 | solution.py:133
  9.1 7.2 %all_gather.9 = bf16[128,1024]{0,1:T(8,128)(2,1)S(1)} all-gather(bf16[128,256]{0,1:T(8,128)(2,1)S(1)} %bitcast_select_fusion.4), channel_id=1, replica_groups=mesh['dp'=4,'section'=2,'mp'=4] {'mp'}, dimensions={1}, use_global_device_ids=true | all-gather | bytes 327680 | tf_op jit(solution)/shard_map/while/body/eval_jaxpr/all_gather | solution.py:120
  16.4 4.1 %conditional.8 = (bf16[128,256]{0,1:T(8,128)(2,1)S(1)}) conditional(s32[]{:T(128)} %convert_element_type.241, () %tuple.133, (bf16[128,1024]{0,1:T(8,128)(2,1)S(1)}, s32[]{:T(128)}, bf16[1024,256]{1,0:T(8,128)(2,1)}, bf16[1024,256]{1,0:T(8,128)(2,1)}, s32[2,128]{1,0:T(2,128)}, /*index=5*/s32[]{:T(128)}, bf16[1024,124]{1,0:T(8,128)(2,1)}) %tuple.134), branch_computations={%region_1.1_spmd, %region_2.5_spmd} | conditional | flops 184088704 | bytes 9459834 | solution.py:122
  24.9 5.8 %all_gather.9 = bf16[128,1024]{0,1:T(8,128)(2,1)S(1)} all-gather(bf16[128,256]{0,1:T(8,128)(2,1)S(1)} %bitcast_select_fusion.4), channel_id=1, replica_groups=mesh['dp'=4,'section'=2,'mp'=4] {'mp'}, dimensions={1}, use_global_device_ids=true | all-gather | bytes 327680 | tf_op jit(solution)/shard_map/while/body/eval_jaxpr/all_gather | solution.py:120
  30.7 4.1 %conditional.8 = (bf16[128,256]{0,1:T(8,128)(2,1)S(1)}) conditional(s32[]{:T(128)} %convert_element_type.241, () %tuple.133, (bf16[128,1024]{0,1:T(8,128)(2,1)S(1)}, s32[]{:T(128)}, bf16[1024,256]{1,0:T(8,128)(2,1)}, bf16[1024,256]{1,0:T(8,128)(2,1)}, s32[2,128]{1,0:T(2,128)}, /*index=5*/s32[]{:T(128)}, bf16[1024,124]{1,0:T(8,128)(2,1)}) %tuple.134), branch_computations={%region_1.1_spmd, %region_2.5_spmd} | conditional | flops 184088704 | bytes 9459834 | solution.py:122
  34.8 4.4 %collective-permute-start = (bf16[128,256]{0,1:T(8,128)(2,1)S(1)}, bf16[128,256]{0,1:T(8,128)(2,1)S(1)}, u32[]{:S(2)}, u32[]{:S(2)}) collective-permute-start(bf16[128,256]{0,1:T(8,128)(2,1)S(1)} %get-tuple-element.1041), channel_id=1, source_target_pairs={{0,4},{1,5},{2,6},{3,7},{8,12},{9,13},{10,14},{11,15},{16,20},{17,... | collective-permute-start | bytes 196616 | tf_op jit(solution)/shard_map/while/body/eval_jaxpr/ppermute | solution.py:12
  42.1 5.8 %all_gather.9 = bf16[128,1024]{0,1:T(8,128)(2,1)S(1)} all-gather(bf16[128,256]{0,1:T(8,128)(2,1)S(1)} %bitcast_select_fusion.4), channel_id=1, replica_groups=mesh['dp'=4,'section'=2,'mp'=4] {'mp'}, dimensions={1}, use_global_device_ids=true | all-gather | bytes 327680 | tf_op jit(solution)/shard_map/while/body/eval_jaxpr/all_gather | solution.py:120
  47.9 8.5 %collective-permute-start = (bf16[128,256]{0,1:T(8,128)(2,1)S(1)}, bf16[128,256]{0,1:T(8,128)(2,1)S(1)}, u32[]{:S(2)}, u32[]{:S(2)}) collective-permute-start(bf16[128,256]{0,1:T(8,128)(2,1)S(1)} %get-tuple-element.1041), channel_id=1, source_target_pairs={{0,4},{1,5},{2,6},{3,7},{8,12},{9,13},{10,14},{11,15},{16,20},{17,... | collective-permute-start | bytes 196616 | tf_op jit(solution)/shard_map/while/body/eval_jaxpr/ppermute | solution.py:12
  59.5 257.4 %while.39 = (s32[]{:T(128)}, f32[128,256]{1,0:T(8,128)}, f32[1024,636]{1,0:T(8,128)S(1)}, s32[]{:T(128)}, pred[]{:T(512)}, /*index=5*/bf16[2,128,256]{2,1,0:T(8,...) while((s32[]{:T(128)}, f32[128,256]{1,0:T(8,128)}, ...), condition=%wide.region_20.21_spmd.clone, body=%wide.region_8.20_spmd.clone.sunk | while | flops 533156512 | bytes 23325744 | solution.py:175
  59.5 1.7 constant_dynamic-slice_fusion.8
  65.9 71.7 %all-reduce.2.cloned.1.call-done = bf16[128,1024]{1,0:T(8,128)(2,1)} async-done(((bf16[128,1024]{1,0:T(8,128)(2,1)}), bf16[128,1024]{1,0:T(8,128)(2,1)}) %all-reduce.2.cloned.1.call-update) | async-done | bytes 262160 | tf_op jit(solution)/shard_map/while/body/eval_jaxpr/psum | solution.py:152
  141.8 4.8 %collective-permute-done.1 = bf16[128,256]{1,0:T(8,128)(2,1)S(1)} collective-permute-done((bf16[128,256]{1,0:T(8,128)(2,1)S(1)}, bf16[128,256]{1,0:T(8,128)(2,1)S(1)}, u32[]{:S(2)}, u32[]{:S(2)}) %collective-permute-start.1) | collective-permute-done | bytes 65568 | tf_op jit(solution)/shard_map/while/body/eval_jaxpr/ppermute | solution.py:12
  147.3 1.7 constant_dynamic-slice_fusion.8
  152.3 38.8 %conditional.9 = (bf16[128,1024]{1,0:T(8,128)(2,1)}, bf16[128,636]{1,0:T(8,128)(2,1)}) conditional(s32[]{:T(128)} %convert_element_type.248, () %tuple.138, (s32[2,128]{1,0:T(2,128)}, s32[]{:T(128)}, bf16[128,1024]{1,0:T(8,128)(2,1)}, bf16[1024,124]{1,0:T(8,128)(2,1)}, f32[128,256]{1,0:T(8,128)S(1)}, /*index=5*/bf16[1024,256]{1,0:T(8,128)(2,1)}, ...), branch_computations={%region_11.11_spmd, %region_12.14_spmd} | conditional | flops 362930720 | bytes 10925676 | solution.py:144
  154.5 1.9 convolution_exponential_fusion.1
  160.7 2.0 fusion.23
  162.8 1.7 copy.31
  166.8 1.6 copy.33
  168.4 2.0 multiply_convert_fusion.4
  170.4 1.6 copy.35
  172.0 1.8 convolution_bitcast_fusion
  173.7 1.7 copy.36
  175.4 1.6 fusion.16
  176.9 7.4 %fusion.20 = bf16[128,4,31]{2,1,0:T(4,128)(2,1)} fusion(f32[128,4,31]{2,1,0:T(4,128)S(1)} %fusion.16, f32[128,4,31]{2,1,0:T(4,128)} %copy.31, f32[128,4]{1,0:T(8,128)} %copy.30), kind=kOutput, calls=%fused_computation.45 | output fusion | flops 95774 | bytes 160768 | tf_op jit(solution)/shard_map/while/body/eval_jaxpr/cond/branch_1_fun/sub | solution.py:84
  184.3 1.7 reshape.248
  186.0 1.6 pad_maximum_fusion
  191.1 31.2 %all-reduce.2.cloned.1.call-done = bf16[128,1024]{1,0:T(8,128)(2,1)} async-done(((bf16[128,1024]{1,0:T(8,128)(2,1)}), bf16[128,1024]{1,0:T(8,128)(2,1)}) %all-reduce.2.cloned.1.call-update) | async-done | bytes 262160 | tf_op jit(solution)/shard_map/while/body/eval_jaxpr/psum | solution.py:152
  226.6 1.7 conditional.10
  226.6 1.7 convolution_add_fusion.2
  228.3 3.1 collective-permute-done.1
  232.1 1.7 constant_dynamic-slice_fusion.8
  237.1 38.8 %conditional.9 = (bf16[128,1024]{1,0:T(8,128)(2,1)}, bf16[128,636]{1,0:T(8,128)(2,1)}) conditional(s32[]{:T(128)} %convert_element_type.248, () %tuple.138, (s32[2,128]{1,0:T(2,128)}, s32[]{:T(128)}, bf16[128,1024]{1,0:T(8,128)(2,1)}, bf16[1024,124]{1,0:T(8,128)(2,1)}, f32[128,256]{1,0:T(8,128)S(1)}, /*index=5*/bf16[1024,256]{1,0:T(8,128)(2,1)}, ...), branch_computations={%region_11.11_spmd, %region_12.14_spmd} | conditional | flops 362930720 | bytes 10925676 | solution.py:144
  239.3 1.9 convolution_exponential_fusion.1
  245.5 2.0 fusion.23
  247.6 1.7 copy.31
  251.6 1.6 copy.33
  253.2 2.0 multiply_convert_fusion.4
  255.2 1.6 copy.35
  256.8 1.8 convolution_bitcast_fusion
  258.5 1.7 copy.36
  261.7 7.4 %fusion.20 = bf16[128,4,31]{2,1,0:T(4,128)(2,1)} fusion(f32[128,4,31]{2,1,0:T(4,128)S(1)} %fusion.16, f32[128,4,31]{2,1,0:T(4,128)} %copy.31, f32[128,4]{1,0:T(8,128)} %copy.30), kind=kOutput, calls=%fused_computation.45 | output fusion | flops 95774 | bytes 160768 | tf_op jit(solution)/shard_map/while/body/eval_jaxpr/cond/branch_1_fun/sub | solution.py:84
  269.1 1.7 reshape.248
  270.8 1.6 pad_maximum_fusion
  275.9 31.2 %all-reduce.2.cloned.1.call-done = bf16[128,1024]{1,0:T(8,128)(2,1)} async-done(((bf16[128,1024]{1,0:T(8,128)(2,1)}), bf16[128,1024]{1,0:T(8,128)(2,1)}) %all-reduce.2.cloned.1.call-update) | async-done | bytes 262160 | tf_op jit(solution)/shard_map/while/body/eval_jaxpr/psum | solution.py:152
  311.4 1.7 conditional.10
  311.4 1.7 convolution_add_fusion.2
  313.1 3.1 collective-permute-done.1
  318.2 31.9 %reduce-scatter.2.cloned.1.call-done = bf16[256,636]{1,0:T(8,128)(2,1)} async-done(((bf16[1024,636]{1,0:T(8,128)(2,1)}), bf16[256,636]{1,0:T(8,128)(2,1)}) %reduce-scatter.2.cloned.1.call-update) | async-done | bytes 325648 | tf_op jit(solution)/shard_map/reduce_scatter | solution.py:178
  (189 shorter events, 76.7 us)
Async XLA Ops:
  16.4 5.5 %copy-start.9 = (s32[3]{0:T(128)S(1)}, s32[3]{0:T(128)}, u32[]{:S(2)}) copy-start(s32[3]{0:T(128)} %get-tuple-element.994) | copy-start | bytes 40 | tf_op jit(solution)/shard_map/while
  16.4 3.2 copy-start
  16.4 3.4 copy-start.5
  20.5 3.4 collective-permute-start
  30.7 8.6 %copy-start.9 = (s32[3]{0:T(128)S(1)}, s32[3]{0:T(128)}, u32[]{:S(2)}) copy-start(s32[3]{0:T(128)} %get-tuple-element.994) | copy-start | bytes 40 | tf_op jit(solution)/shard_map/while
  30.7 3.2 copy-start
  30.7 3.4 copy-start.5
  34.8 6.3 %collective-permute-start = (bf16[128,256]{0,1:T(8,128)(2,1)S(1)}, bf16[128,256]{0,1:T(8,128)(2,1)S(1)}, u32[]{:S(2)}, u32[]{:S(2)}) collective-permute-start(bf16[128,256]{0,1:T(8,128)(2,1)S(1)} %get-tuple-element.1041), channel_id=1, source_target_pairs={{0,4},{1,5},{2,6},{3,7},{8,12},{9,13},{10,14},{11,15},{16,20},{17,... | collective-permute-start | bytes 196616 | tf_op jit(solution)/shard_map/while/body/eval_jaxpr/ppermute | solution.py:12
  47.9 8.5 %copy-start.9 = (s32[3]{0:T(128)S(1)}, s32[3]{0:T(128)}, u32[]{:S(2)}) copy-start(s32[3]{0:T(128)} %get-tuple-element.994) | copy-start | bytes 40 | tf_op jit(solution)/shard_map/while
  47.9 10.4 %collective-permute-start = (bf16[128,256]{0,1:T(8,128)(2,1)S(1)}, bf16[128,256]{0,1:T(8,128)(2,1)S(1)}, u32[]{:S(2)}, u32[]{:S(2)}) collective-permute-start(bf16[128,256]{0,1:T(8,128)(2,1)S(1)} %get-tuple-element.1041), channel_id=1, source_target_pairs={{0,4},{1,5},{2,6},{3,7},{8,12},{9,13},{10,14},{11,15},{16,20},{17,... | collective-permute-start | bytes 196616 | tf_op jit(solution)/shard_map/while/body/eval_jaxpr/ppermute | solution.py:12
  58.3 0.8 copy-start.3
  58.3 1.2 copy-start.1
  59.5 78.1 %all-reduce.2.cloned.1.call-start = ((), (), s32[]{:S(2)}) async-start(), calls=%async_computation.2 | async-start | bytes 524288 | tf_op jit(solution)/shard_map/while/body/eval_jaxpr/psum | solution.py:152
  62.4 1.2 copy-start.7
  62.6 0.9 copy-start.8
  140.5 6.2 %collective-permute-start.1 = (bf16[128,256]{1,0:T(8,128)(2,1)S(1)}, bf16[128,256]{1,0:T(8,128)(2,1)S(1)}, u32[]{:S(2)}, u32[]{:S(2)}) collective-permute-start(bf16[128,256]{1,0:T(8,128)(2,1)S(1)} %fusion.74), channel_id=1, source_target_pairs={{4,0},{5,1},{6,2},{7,3},{12,8},{13,9},{14,10},{15,11},{20,16},{21,... | collective-permute-start | bytes 196616 | tf_op jit(solution)/shard_map/while/body/eval_jaxpr/ppermute | solution.py:12
  147.3 75.0 %all-reduce.2.cloned.1.call-start = ((), (), s32[]{:S(2)}) async-start(), calls=%async_computation.2 | async-start | bytes 524288 | tf_op jit(solution)/shard_map/while/body/eval_jaxpr/psum | solution.py:152
  150.2 1.2 copy-start.7
  150.5 0.9 copy-start.8
  164.4 1.5 copy-start.4
  186.0 4.2 %copy-start.2 = (bf16[1024,124]{1,0:T(8,128)(2,1)S(1)}, bf16[1024,124]{1,0:T(8,128)(2,1)}, u32[]{:S(2)}) copy-start(bf16[1024,124]{1,0:T(8,128)(2,1)} %get-tuple-element.579) | copy-start | bytes 761860 | tf_op jit(solution)/shard_map/while/body/eval_jaxpr/cond
  186.0 4.2 %copy-start.6 = (bf16[128,124]{1,0:T(8,128)(2,1)S(1)}, bf16[128,124]{1,0:T(8,128)(2,1)}, u32[]{:S(2)}) copy-start(bf16[128,124]{1,0:T(8,128)(2,1)} %reshape.248) | copy-start | bytes 95236 | tf_op jit(solution)/shard_map/while/body/eval_jaxpr/cond
  225.3 6.2 %collective-permute-start.1 = (bf16[128,256]{1,0:T(8,128)(2,1)S(1)}, bf16[128,256]{1,0:T(8,128)(2,1)S(1)}, u32[]{:S(2)}, u32[]{:S(2)}) collective-permute-start(bf16[128,256]{1,0:T(8,128)(2,1)S(1)} %fusion.74), channel_id=1, source_target_pairs={{4,0},{5,1},{6,2},{7,3},{12,8},{13,9},{14,10},{15,11},{20,16},{21,... | collective-permute-start | bytes 196616 | tf_op jit(solution)/shard_map/while/body/eval_jaxpr/ppermute | solution.py:12
  232.1 75.0 %all-reduce.2.cloned.1.call-start = ((), (), s32[]{:S(2)}) async-start(), calls=%async_computation.2 | async-start | bytes 524288 | tf_op jit(solution)/shard_map/while/body/eval_jaxpr/psum | solution.py:152
  235.0 1.2 copy-start.7
  235.3 0.9 copy-start.8
  249.2 1.5 copy-start.4
  270.8 4.2 %copy-start.2 = (bf16[1024,124]{1,0:T(8,128)(2,1)S(1)}, bf16[1024,124]{1,0:T(8,128)(2,1)}, u32[]{:S(2)}) copy-start(bf16[1024,124]{1,0:T(8,128)(2,1)} %get-tuple-element.579) | copy-start | bytes 761860 | tf_op jit(solution)/shard_map/while/body/eval_jaxpr/cond
  270.8 4.2 %copy-start.6 = (bf16[128,124]{1,0:T(8,128)(2,1)S(1)}, bf16[128,124]{1,0:T(8,128)(2,1)}, u32[]{:S(2)}) copy-start(bf16[128,124]{1,0:T(8,128)(2,1)} %reshape.248) | copy-start | bytes 95236 | tf_op jit(solution)/shard_map/while/body/eval_jaxpr/cond
  310.1 6.2 %collective-permute-start.1 = (bf16[128,256]{1,0:T(8,128)(2,1)S(1)}, bf16[128,256]{1,0:T(8,128)(2,1)S(1)}, u32[]{:S(2)}, u32[]{:S(2)}) collective-permute-start(bf16[128,256]{1,0:T(8,128)(2,1)S(1)} %fusion.74), channel_id=1, source_target_pairs={{4,0},{5,1},{6,2},{7,3},{12,8},{13,9},{14,10},{15,11},{20,16},{21,... | collective-permute-start | bytes 196616 | tf_op jit(solution)/shard_map/while/body/eval_jaxpr/ppermute | solution.py:12
  316.9 33.1 %reduce-scatter.2.cloned.1.call-start = ((), (), s32[]{:S(2)}) async-start(), calls=%async_computation.1 | async-start | bytes 1638400 | tf_op jit(solution)/shard_map/reduce_scatter | solution.py:178
Sparse Core Ops, SparseCore 0:
  66.0 71.5 all-reduce.1
  191.3 31.0 all-reduce.1
  276.0 31.0 all-reduce.1
Sparse Core Ops, SparseCore 1:
  319.7 30.3 reduce-scatter.1
where the time goes:
time: 362 us; the launch traced here: 360 us
  waiting for transfers between devices  179 us (49%)
  other arithmetic  47.1 us (13%)
  local copies, waits for them, and re-layouts  42.7 us (12%)
  matrix products  38.4 us (11%)
  blocking collectives  18.8 us (5%)
  starting transfers between devices  18 us (5%)
  between operations  15.2 us (4%)
    psum x3, waiting for transfers between devices, backward_tick(): lax.psum(grad_part.astype(jnp.bfloat16), 'mp').astype(jnp.float32)  134 us
    reduce_scatter x1, waiting for transfers between devices, shards(): lax.psum_scatter(grads.astype(jnp.bfloat16), 'dp', scatter_dimension=0, t...  31.9 us
    all_gather x3, blocking collectives, forward_tick(): full_rows = lax.all_gather(own_rows, 'mp', axis=1, tiled=True)  18.8 us
    ppermute x6, starting transfers between devices, from_behind(): lax.ppermute(value, axis, [(source, source + steps) for source in range(i...  18 us
    sub x2, other arithmetic, layer_backward(): grad_taps - jnp.sum(taps * grad_taps, axis=-1, keepdims=True)  14.8 us
    ppermute x6, waiting for transfers between devices, from_behind(): lax.ppermute(value, axis, [(source, source + steps) for source in range(i...  12.7 us
    dynamic_slice x6, local copies, waits for them, and re-layouts, backward_tick(): normed, inv_std, normed_b = normalize(stored[slot_index])  8.26 us
  transfers between devices with their start and end apart: 10, of which 10 were waited for; matrix products, arithmetic and copies ran while one was open for 2% of the time, Pallas kernels for 0%

commit v1 on v0

--- a/solution.py
+++ b/solution.py
@@ -117,7 +117,14 @@
         active = (micro_index >= 0) & (micro_index < micro_count)
         slot_index = jnp.clip(micro_index, 0, micro_count - 1)
         own_rows = jnp.where(section_index == 0, inputs[slot_index], received)
-        full_rows = lax.all_gather(own_rows, "mp", axis=1, tiled=True)
+        ring = [own_rows]
+        for hop in range(3):
+            ring.append(lax.ppermute(ring[-1], "mp", [(dev, (dev + 1) % 4) for dev in range(4)]))
+        full_rows = jnp.roll(
+            jnp.concatenate(ring[::-1], axis=1),
+            (lax.axis_index("mp") + 1) * ring[0].shape[1],
+            axis=1,
+        )
         segments = segment_ids[slot_index]
         result = lax.cond(
             active,

time: 362 us -> 376 us (1.039)
  waiting for transfers between devices: 179 us -> 212 us
  blocking collectives: 18.8 us -> 0 us
    ppermute x0 -> x9, waiting for transfers between devices: none -> 28.8 us  [forward_tick(): lax.ppermute(ring[-1], 'mp', [(dev, (dev + 1) % 4) for dev in range(4)])]
    all_gather x3 -> x0, blocking collectives: 18.8 us -> none  [forward_tick(): full_rows = lax.all_gather(own_rows, 'mp', axis=1, tiled=True)]
    ppermute x6, waiting for transfers between devices: 12.7 us -> 16.7 us  [from_behind(): lax.ppermute(value, axis, [(source, source + steps) for source in range(i...]
  transfers between devices with their start and end apart: 10 -> 19, of which waited for: 10 -> 19; matrix products, arithmetic and copies ran while one was open for 2% -> 2% of each run, Pallas kernels for 0% -> 0%
where the time goes in v1:
time: 376 us; the launch traced here: 374 us
  waiting for transfers between devices  212 us (56%)
  other arithmetic  49.8 us (13%)
  local copies, waits for them, and re-layouts  41.8 us (11%)
  matrix products  36.5 us (10%)
  starting transfers between devices  17.4 us (5%)
  between operations  15.2 us (4%)
    psum x3, waiting for transfers between devices, backward_tick(): lax.psum(grad_part.astype(jnp.bfloat16), 'mp').astype(jnp.float32)  134 us
    reduce_scatter x1, waiting for transfers between devices, shards(): lax.psum_scatter(grads.astype(jnp.bfloat16), 'dp', scatter_dimension=0, t...  31.9 us
    ppermute x9, waiting for transfers between devices, forward_tick(): lax.ppermute(ring[-1], 'mp', [(dev, (dev + 1) % 4) for dev in range(4)])  28.8 us
    ppermute x6, waiting for transfers between devices, from_behind(): lax.ppermute(value, axis, [(source, source + steps) for source in range(i...  16.7 us
    ppermute x6, starting transfers between devices, from_behind(): lax.ppermute(value, axis, [(source, source + steps) for source in range(i...  16.6 us
    sub x2, other arithmetic, layer_backward(): grad_taps - jnp.sum(taps * grad_taps, axis=-1, keepdims=True)  14.8 us
    dynamic_slice x6, local copies, waits for them, and re-layouts, backward_tick(): normed, inv_std, normed_b = normalize(stored[slot_index])  8.26 us
  transfers between devices with their start and end apart: 19, of which 19 were waited for; matrix products, arithmetic and copies ran while one was open for 2% of the time, Pallas kernels for 0%

profile of v1, /device:TPU:0, one launch (start us, length us, event | category | flops | bytes accessed | tf_op | source)
XLA Modules:
  0.0 373.6 jit_solution(9869580517176159733)
XLA Ops:
  8.1 63.7 %while.39 = (s32[]{:T(128)}, bf16[128,256]{0,1:T(8,128)(2,1)S(1)}, bf16[2,128,1024]{1,2,0:T(8,128)(2,1)S(1)}, s32[]{:T(128)}, pred[]{:T(512)}, /*index=5*/bf16[2...) while((s32[]{:T(128)}, bf16[128,256]{0,1:T(8,128)(2,1)S(1)}, ...), condition=%wide.region_7.8_spmd, body=%wide.region_0.7_spmd.sunk | while | flops 184383664 | bytes 14609268 | solution.py:140
  9.8 3.9 %collective-permute-done = bf16[128,256]{0,1:T(8,128)(2,1)S(1)} collective-permute-done((bf16[128,256]{0,1:T(8,128)(2,1)S(1)}, bf16[128,256]{0,1:T(8,128)(2,1)S(1)}, u32[]{:S(2)}, u32[]{:S(2)}) %collective-permute-start) | collective-permute-done | bytes 65568 | tf_op jit(solution)/shard_map/while/body/eval_jaxpr/ppermute | solution.py:122
  13.8 3.6 collective-permute-done.1
  18.9 2.2 collective-permute-done.2
  22.1 2.4 conditional.8
  24.5 1.8 collective-permute-start.3
  26.3 1.9 collective-permute-done.3
  29.4 3.6 collective-permute-done
  33.0 3.7 collective-permute-done.1
  38.2 2.2 collective-permute-done.2
  41.4 2.4 conditional.8
  43.8 4.3 %collective-permute-start.3 = (bf16[128,256]{0,1:T(8,128)(2,1)S(1)}, bf16[128,256]{0,1:T(8,128)(2,1)S(1)}, u32[]{:S(2)}, u32[]{:S(2)}) collective-permute-start(bf16[128,256]{0,1:T(8,128)(2,1)S(1)} %get-tuple-element.1100), channel_id=1, source_target_pairs={{0,4},{1,5},{2,6},{3,7},{8,12},{9,13},{10,14},{11,15},{16,20},{17,... | collective-permute-start | bytes 196616 | tf_op jit(solution)/shard_map/while/body/eval_jaxpr/ppermute | solution.py:12
  48.1 1.9 collective-permute-done.3
  51.2 3.6 collective-permute-done
  54.9 3.7 collective-permute-done.1
  60.0 2.2 collective-permute-done.2
  63.3 6.7 %collective-permute-start.3 = (bf16[128,256]{0,1:T(8,128)(2,1)S(1)}, bf16[128,256]{0,1:T(8,128)(2,1)S(1)}, u32[]{:S(2)}, u32[]{:S(2)}) collective-permute-start(bf16[128,256]{0,1:T(8,128)(2,1)S(1)} %get-tuple-element.1100), channel_id=1, source_target_pairs={{0,4},{1,5},{2,6},{3,7},{8,12},{9,13},{10,14},{11,15},{16,20},{17,... | collective-permute-start | bytes 196616 | tf_op jit(solution)/shard_map/while/body/eval_jaxpr/ppermute | solution.py:12
  70.0 1.9 collective-permute-done.3
  73.1 257.6 %while.40 = (s32[]{:T(128)}, f32[128,256]{1,0:T(8,128)}, f32[1024,636]{1,0:T(8,128)S(1)}, s32[]{:T(128)}, pred[]{:T(512)}, /*index=5*/bf16[2,128,256]{2,1,0:T(8,...) while((s32[]{:T(128)}, f32[128,256]{1,0:T(8,128)}, ...), condition=%wide.region_20.21_spmd.clone, body=%wide.region_8.20_spmd.clone.sunk | while | flops 533156512 | bytes 23325744 | solution.py:182
  73.1 1.7 constant_dynamic-slice_fusion.10
  79.5 71.9 %all-reduce.2.cloned.1.call-done = bf16[128,1024]{1,0:T(8,128)(2,1)} async-done(((bf16[128,1024]{1,0:T(8,128)(2,1)}), bf16[128,1024]{1,0:T(8,128)(2,1)}) %all-reduce.2.cloned.1.call-update) | async-done | bytes 262160 | tf_op jit(solution)/shard_map/while/body/eval_jaxpr/psum | solution.py:159
  155.6 4.8 %collective-permute-done.4 = bf16[128,256]{1,0:T(8,128)(2,1)S(1)} collective-permute-done((bf16[128,256]{1,0:T(8,128)(2,1)S(1)}, bf16[128,256]{1,0:T(8,128)(2,1)S(1)}, u32[]{:S(2)}, u32[]{:S(2)}) %collective-permute-start.4) | collective-permute-done | bytes 65568 | tf_op jit(solution)/shard_map/while/body/eval_jaxpr/ppermute | solution.py:12
  161.1 1.7 constant_dynamic-slice_fusion.10
  166.1 38.8 %conditional.9 = (bf16[128,1024]{1,0:T(8,128)(2,1)}, bf16[128,636]{1,0:T(8,128)(2,1)}) conditional(s32[]{:T(128)} %convert_element_type.250, () %tuple.145, (s32[2,128]{1,0:T(2,128)}, s32[]{:T(128)}, bf16[128,1024]{1,0:T(8,128)(2,1)}, bf16[1024,124]{1,0:T(8,128)(2,1)}, f32[128,256]{1,0:T(8,128)S(1)}, /*index=5*/bf16[1024,256]{1,0:T(8,128)(2,1)}, ...), branch_computations={%region_11.11_spmd, %region_12.14_spmd} | conditional | flops 362930720 | bytes 10925676 | solution.py:151
  168.3 1.9 convolution_exponential_fusion.1
  174.5 2.0 fusion.23
  176.6 1.7 copy.31
  182.2 2.0 multiply_convert_fusion.4
  185.8 1.8 convolution_bitcast_fusion
  190.7 7.4 %fusion.20 = bf16[128,4,31]{2,1,0:T(4,128)(2,1)} fusion(f32[128,4,31]{2,1,0:T(4,128)S(1)} %fusion.16, f32[128,4,31]{2,1,0:T(4,128)} %copy.31, f32[128,4]{1,0:T(8,128)} %copy.30), kind=kOutput, calls=%fused_computation.54 | output fusion | flops 95774 | bytes 160768 | tf_op jit(solution)/shard_map/while/body/eval_jaxpr/cond/branch_1_fun/sub | solution.py:84
  204.9 31.2 %all-reduce.2.cloned.1.call-done = bf16[128,1024]{1,0:T(8,128)(2,1)} async-done(((bf16[128,1024]{1,0:T(8,128)(2,1)}), bf16[128,1024]{1,0:T(8,128)(2,1)}) %all-reduce.2.cloned.1.call-update) | async-done | bytes 262160 | tf_op jit(solution)/shard_map/while/body/eval_jaxpr/psum | solution.py:159
  240.4 1.7 conditional.10
  240.4 1.7 convolution_add_fusion.2
  242.2 3.1 collective-permute-done.4
  245.9 1.7 constant_dynamic-slice_fusion.10
  250.9 38.8 %conditional.9 = (bf16[128,1024]{1,0:T(8,128)(2,1)}, bf16[128,636]{1,0:T(8,128)(2,1)}) conditional(s32[]{:T(128)} %convert_element_type.250, () %tuple.145, (s32[2,128]{1,0:T(2,128)}, s32[]{:T(128)}, bf16[128,1024]{1,0:T(8,128)(2,1)}, bf16[1024,124]{1,0:T(8,128)(2,1)}, f32[128,256]{1,0:T(8,128)S(1)}, /*index=5*/bf16[1024,256]{1,0:T(8,128)(2,1)}, ...), branch_computations={%region_11.11_spmd, %region_12.14_spmd} | conditional | flops 362930720 | bytes 10925676 | solution.py:151
  253.1 1.9 convolution_exponential_fusion.1
  259.4 2.0 fusion.23
  261.4 1.7 copy.31
  267.1 2.0 multiply_convert_fusion.4
  270.6 1.8 convolution_bitcast_fusion
  272.3 1.7 copy.36
  275.6 7.4 %fusion.20 = bf16[128,4,31]{2,1,0:T(4,128)(2,1)} fusion(f32[128,4,31]{2,1,0:T(4,128)S(1)} %fusion.16, f32[128,4,31]{2,1,0:T(4,128)} %copy.31, f32[128,4]{1,0:T(8,128)} %copy.30), kind=kOutput, calls=%fused_computation.54 | output fusion | flops 95774 | bytes 160768 | tf_op jit(solution)/shard_map/while/body/eval_jaxpr/cond/branch_1_fun/sub | solution.py:84
  289.8 31.2 %all-reduce.2.cloned.1.call-done = bf16[128,1024]{1,0:T(8,128)(2,1)} async-done(((bf16[128,1024]{1,0:T(8,128)(2,1)}), bf16[128,1024]{1,0:T(8,128)(2,1)}) %all-reduce.2.cloned.1.call-update) | async-done | bytes 262160 | tf_op jit(solution)/shard_map/while/body/eval_jaxpr/psum | solution.py:159
  325.2 1.7 conditional.10
  325.2 1.7 convolution_add_fusion.2
  326.9 3.1 collective-permute-done.4
  332.0 31.9 %reduce-scatter.2.cloned.1.call-done = bf16[256,636]{1,0:T(8,128)(2,1)} async-done(((bf16[1024,636]{1,0:T(8,128)(2,1)}), bf16[256,636]{1,0:T(8,128)(2,1)}) %reduce-scatter.2.cloned.1.call-update) | async-done | bytes 325648 | tf_op jit(solution)/shard_map/reduce_scatter | solution.py:185
  (238 shorter events, 90.6 us)
Async XLA Ops:
  8.1 13.9 %copy-start = (bf16[1024,256]{1,0:T(8,128)(2,1)S(1)}, bf16[1024,256]{1,0:T(8,128)(2,1)}, u32[]{:S(2)}) copy-start(bf16[1024,256]{1,0:T(8,128)(2,1)} %get-tuple-element.1041) | copy-start | bytes 1572868 | tf_op jit(solution)/shard_map/while
  8.1 13.9 %copy-start.2 = (bf16[1024,124]{1,0:T(8,128)(2,1)S(1)}, bf16[1024,124]{1,0:T(8,128)(2,1)}, u32[]{:S(2)}) copy-start(bf16[1024,124]{1,0:T(8,128)(2,1)} %get-tuple-element.1044) | copy-start | bytes 761860 | tf_op jit(solution)/shard_map/while
  8.2 13.9 %copy-start.6 = (bf16[1024,256]{1,0:T(8,128)(2,1)S(1)}, bf16[1024,256]{1,0:T(8,128)(2,1)}, u32[]{:S(2)}) copy-start(bf16[1024,256]{1,0:T(8,128)(2,1)} %get-tuple-element.1042) | copy-start | bytes 1572868 | tf_op jit(solution)/shard_map/while
  8.2 13.9 %copy-start.10 = (s32[2,128]{1,0:T(2,128)S(1)}, s32[2,128]{1,0:T(2,128)}, u32[]{:S(2)}) copy-start(s32[2,128]{1,0:T(2,128)} %get-tuple-element.1043) | copy-start | bytes 3076 | tf_op jit(solution)/shard_map/while
  9.3 4.4 %collective-permute-start = (bf16[128,256]{0,1:T(8,128)(2,1)S(1)}, bf16[128,256]{0,1:T(8,128)(2,1)S(1)}, u32[]{:S(2)}, u32[]{:S(2)}) collective-permute-start(bf16[128,256]{0,1:T(8,128)(2,1)S(1)} %bitcast_select_fusion.4), channel_id=1, source_target_pairs={{0,1},{1,2},{2,3},{3,0},{4,5},{5,6},{6,7},{7,4},{8,9},{9,10},{10,1... | collective-permute-start | bytes 196616 | tf_op jit(solution)/shard_map/while/body/eval_jaxpr/ppermute | solution.py:122
  13.7 3.7 collective-permute-start.1
  17.4 3.7 collective-permute-start.2
  24.5 3.7 collective-permute-start.3
  28.2 13.2 %copy-start = (bf16[1024,256]{1,0:T(8,128)(2,1)S(1)}, bf16[1024,256]{1,0:T(8,128)(2,1)}, u32[]{:S(2)}) copy-start(bf16[1024,256]{1,0:T(8,128)(2,1)} %get-tuple-element.1041) | copy-start | bytes 1572868 | tf_op jit(solution)/shard_map/while
  28.2 13.2 %copy-start.2 = (bf16[1024,124]{1,0:T(8,128)(2,1)S(1)}, bf16[1024,124]{1,0:T(8,128)(2,1)}, u32[]{:S(2)}) copy-start(bf16[1024,124]{1,0:T(8,128)(2,1)} %get-tuple-element.1044) | copy-start | bytes 761860 | tf_op jit(solution)/shard_map/while
  28.2 13.2 %copy-start.6 = (bf16[1024,256]{1,0:T(8,128)(2,1)S(1)}, bf16[1024,256]{1,0:T(8,128)(2,1)}, u32[]{:S(2)}) copy-start(bf16[1024,256]{1,0:T(8,128)(2,1)} %get-tuple-element.1042) | copy-start | bytes 1572868 | tf_op jit(solution)/shard_map/while
  28.2 13.2 %copy-start.10 = (s32[2,128]{1,0:T(2,128)S(1)}, s32[2,128]{1,0:T(2,128)}, u32[]{:S(2)}) copy-start(s32[2,128]{1,0:T(2,128)} %get-tuple-element.1043) | copy-start | bytes 3076 | tf_op jit(solution)/shard_map/while
  29.3 3.7 %collective-permute-start = (bf16[128,256]{0,1:T(8,128)(2,1)S(1)}, bf16[128,256]{0,1:T(8,128)(2,1)S(1)}, u32[]{:S(2)}, u32[]{:S(2)}) collective-permute-start(bf16[128,256]{0,1:T(8,128)(2,1)S(1)} %bitcast_select_fusion.4), channel_id=1, source_target_pairs={{0,1},{1,2},{2,3},{3,0},{4,5},{5,6},{6,7},{7,4},{8,9},{9,10},{10,1... | collective-permute-start | bytes 196616 | tf_op jit(solution)/shard_map/while/body/eval_jaxpr/ppermute | solution.py:122
  33.0 3.7 collective-permute-start.1
  36.7 3.7 collective-permute-start.2
  43.8 6.2 %collective-permute-start.3 = (bf16[128,256]{0,1:T(8,128)(2,1)S(1)}, bf16[128,256]{0,1:T(8,128)(2,1)S(1)}, u32[]{:S(2)}, u32[]{:S(2)}) collective-permute-start(bf16[128,256]{0,1:T(8,128)(2,1)S(1)} %get-tuple-element.1100), channel_id=1, source_target_pairs={{0,4},{1,5},{2,6},{3,7},{8,12},{9,13},{10,14},{11,15},{16,20},{17,... | collective-permute-start | bytes 196616 | tf_op jit(solution)/shard_map/while/body/eval_jaxpr/ppermute | solution.py:12
  50.0 13.2 %copy-start = (bf16[1024,256]{1,0:T(8,128)(2,1)S(1)}, bf16[1024,256]{1,0:T(8,128)(2,1)}, u32[]{:S(2)}) copy-start(bf16[1024,256]{1,0:T(8,128)(2,1)} %get-tuple-element.1041) | copy-start | bytes 1572868 | tf_op jit(solution)/shard_map/while
  50.0 13.2 %copy-start.2 = (bf16[1024,124]{1,0:T(8,128)(2,1)S(1)}, bf16[1024,124]{1,0:T(8,128)(2,1)}, u32[]{:S(2)}) copy-start(bf16[1024,124]{1,0:T(8,128)(2,1)} %get-tuple-element.1044) | copy-start | bytes 761860 | tf_op jit(solution)/shard_map/while
  50.0 13.2 %copy-start.6 = (bf16[1024,256]{1,0:T(8,128)(2,1)S(1)}, bf16[1024,256]{1,0:T(8,128)(2,1)}, u32[]{:S(2)}) copy-start(bf16[1024,256]{1,0:T(8,128)(2,1)} %get-tuple-element.1042) | copy-start | bytes 1572868 | tf_op jit(solution)/shard_map/while
  50.0 13.2 %copy-start.10 = (s32[2,128]{1,0:T(2,128)S(1)}, s32[2,128]{1,0:T(2,128)}, u32[]{:S(2)}) copy-start(s32[2,128]{1,0:T(2,128)} %get-tuple-element.1043) | copy-start | bytes 3076 | tf_op jit(solution)/shard_map/while
  51.1 3.7 %collective-permute-start = (bf16[128,256]{0,1:T(8,128)(2,1)S(1)}, bf16[128,256]{0,1:T(8,128)(2,1)S(1)}, u32[]{:S(2)}, u32[]{:S(2)}) collective-permute-start(bf16[128,256]{0,1:T(8,128)(2,1)S(1)} %bitcast_select_fusion.4), channel_id=1, source_target_pairs={{0,1},{1,2},{2,3},{3,0},{4,5},{5,6},{6,7},{7,4},{8,9},{9,10},{10,1... | collective-permute-start | bytes 196616 | tf_op jit(solution)/shard_map/while/body/eval_jaxpr/ppermute | solution.py:122
  54.8 3.7 collective-permute-start.1
  58.5 3.7 collective-permute-start.2
  63.3 8.6 %collective-permute-start.3 = (bf16[128,256]{0,1:T(8,128)(2,1)S(1)}, bf16[128,256]{0,1:T(8,128)(2,1)S(1)}, u32[]{:S(2)}, u32[]{:S(2)}) collective-permute-start(bf16[128,256]{0,1:T(8,128)(2,1)S(1)} %get-tuple-element.1100), channel_id=1, source_target_pairs={{0,4},{1,5},{2,6},{3,7},{8,12},{9,13},{10,14},{11,15},{16,20},{17,... | collective-permute-start | bytes 196616 | tf_op jit(solution)/shard_map/while/body/eval_jaxpr/ppermute | solution.py:12
  71.8 0.8 copy-start.4
  71.8 1.2 copy-start.1
  73.1 78.3 %all-reduce.2.cloned.1.call-start = ((), (), s32[]{:S(2)}) async-start(), calls=%async_computation.2 | async-start | bytes 524288 | tf_op jit(solution)/shard_map/while/body/eval_jaxpr/psum | solution.py:159
  76.0 2.0 copy-start.8
  76.2 1.8 copy-start.9
  154.3 6.2 %collective-permute-start.4 = (bf16[128,256]{1,0:T(8,128)(2,1)S(1)}, bf16[128,256]{1,0:T(8,128)(2,1)S(1)}, u32[]{:S(2)}, u32[]{:S(2)}) collective-permute-start(bf16[128,256]{1,0:T(8,128)(2,1)S(1)} %fusion.74), channel_id=1, source_target_pairs={{4,0},{5,1},{6,2},{7,3},{12,8},{13,9},{14,10},{15,11},{20,16},{21,... | collective-permute-start | bytes 196616 | tf_op jit(solution)/shard_map/while/body/eval_jaxpr/ppermute | solution.py:12
  161.1 75.0 %all-reduce.2.cloned.1.call-start = ((), (), s32[]{:S(2)}) async-start(), calls=%async_computation.2 | async-start | bytes 524288 | tf_op jit(solution)/shard_map/while/body/eval_jaxpr/psum | solution.py:159
  164.0 2.1 copy-start.8
  164.3 1.9 copy-start.9
  178.3 1.5 copy-start.5
  199.8 4.2 %copy-start.3 = (bf16[1024,124]{1,0:T(8,128)(2,1)S(1)}, bf16[1024,124]{1,0:T(8,128)(2,1)}, u32[]{:S(2)}) copy-start(bf16[1024,124]{1,0:T(8,128)(2,1)} %get-tuple-element.617) | copy-start | bytes 761860 | tf_op jit(solution)/shard_map/while/body/eval_jaxpr/cond
  199.8 4.2 %copy-start.7 = (bf16[128,124]{1,0:T(8,128)(2,1)S(1)}, bf16[128,124]{1,0:T(8,128)(2,1)}, u32[]{:S(2)}) copy-start(bf16[128,124]{1,0:T(8,128)(2,1)} %reshape.252) | copy-start | bytes 95236 | tf_op jit(solution)/shard_map/while/body/eval_jaxpr/cond
  239.1 6.2 %collective-permute-start.4 = (bf16[128,256]{1,0:T(8,128)(2,1)S(1)}, bf16[128,256]{1,0:T(8,128)(2,1)S(1)}, u32[]{:S(2)}, u32[]{:S(2)}) collective-permute-start(bf16[128,256]{1,0:T(8,128)(2,1)S(1)} %fusion.74), channel_id=1, source_target_pairs={{4,0},{5,1},{6,2},{7,3},{12,8},{13,9},{14,10},{15,11},{20,16},{21,... | collective-permute-start | bytes 196616 | tf_op jit(solution)/shard_map/while/body/eval_jaxpr/ppermute | solution.py:12
  245.9 75.0 %all-reduce.2.cloned.1.call-start = ((), (), s32[]{:S(2)}) async-start(), calls=%async_computation.2 | async-start | bytes 524288 | tf_op jit(solution)/shard_map/while/body/eval_jaxpr/psum | solution.py:159
  248.8 2.1 copy-start.8
  249.1 1.9 copy-start.9
  263.1 1.5 copy-start.5
  284.6 4.2 %copy-start.3 = (bf16[1024,124]{1,0:T(8,128)(2,1)S(1)}, bf16[1024,124]{1,0:T(8,128)(2,1)}, u32[]{:S(2)}) copy-start(bf16[1024,124]{1,0:T(8,128)(2,1)} %get-tuple-element.617) | copy-start | bytes 761860 | tf_op jit(solution)/shard_map/while/body/eval_jaxpr/cond
  284.6 4.2 %copy-start.7 = (bf16[128,124]{1,0:T(8,128)(2,1)S(1)}, bf16[128,124]{1,0:T(8,128)(2,1)}, u32[]{:S(2)}) copy-start(bf16[128,124]{1,0:T(8,128)(2,1)} %reshape.252) | copy-start | bytes 95236 | tf_op jit(solution)/shard_map/while/body/eval_jaxpr/cond
  323.9 6.2 %collective-permute-start.4 = (bf16[128,256]{1,0:T(8,128)(2,1)S(1)}, bf16[128,256]{1,0:T(8,128)(2,1)S(1)}, u32[]{:S(2)}, u32[]{:S(2)}) collective-permute-start(bf16[128,256]{1,0:T(8,128)(2,1)S(1)} %fusion.74), channel_id=1, source_target_pairs={{4,0},{5,1},{6,2},{7,3},{12,8},{13,9},{14,10},{15,11},{20,16},{21,... | collective-permute-start | bytes 196616 | tf_op jit(solution)/shard_map/while/body/eval_jaxpr/ppermute | solution.py:12
  330.7 33.1 %reduce-scatter.2.cloned.1.call-start = ((), (), s32[]{:S(2)}) async-start(), calls=%async_computation.1 | async-start | bytes 1638400 | tf_op jit(solution)/shard_map/reduce_scatter | solution.py:185
Sparse Core Ops, SparseCore 0:
  79.6 71.7 all-reduce.1
  205.1 31.0 all-reduce.1
  289.9 31.0 all-reduce.1
Sparse Core Ops, SparseCore 1:
  333.5 30.3 reduce-scatter.1
